TPU v7x, 128 devices: a whole 4x4x4 slice. The times are simulated.
128 devices in a mesh: role: 2 (over core), dev: 64 (over z, y, x).
Axes of the slice: x: 4, y: 4, z: 4, core: 2. Of those that a mesh axis runs over, the one named last changes fastest.
Arguments:
- moe_rows: bfloat16 [4096, 3584], P(('role', 'dev')), may hold values from -6 to 6
- expert_ids: int32 [4096, 8], P(('role', 'dev')), may hold values from 0 to 63, all different within a row; in each aligned block of 32 rows (0 to 31, 32 to 63, ...) at most 8 rows name the same one
- gate_weights: float32 [4096, 8], P(('role', 'dev')), may hold values from 0.05 to 0.6
- w_gate: bfloat16 [64, 3584, 1024], P('dev', None, 'role'), may hold values from -0.09375 to 0.09375
- w_up: bfloat16 [64, 3584, 1024], P('dev', None, 'role'), may hold values from -0.09375 to 0.09375
- w_down: bfloat16 [64, 3584, 1024], P('dev', None, 'role'), may hold values from -0.1875 to 0.1875
- q_latent: bfloat16 [512, 64, 512], P(('role', 'dev')), may hold values from -40 to 40
- q_rope: bfloat16 [512, 4096], P(('role', 'dev')), may hold values from -4 to 4
- latent_cache: bfloat16 [512, 2048, 512], P(('role', 'dev')), may hold values from -4 to 4
- rope_cache: bfloat16 [512, 64, 2048], P(('role', 'dev')), may hold values from -4 to 4
- lengths: int32 [512], P(('role', 'dev')), may hold values from 2 to 2048, as said below
Outputs:
- moe_out: bfloat16 [4096, 3584], P(('role', 'dev'))
- attended: bfloat16 [512, 64, 512], P(('role', 'dev'))
Inputs may be any that keep to these rules, and one draw needn't show every extreme that they name: `expert_ids`: each row names 8 different experts; among the rows of one device no expert is named more than 8 times. `lengths`: the first row holds all 2048 cached tokens.
All inputs are finite; a program needn't handle non-finite values.
Results may differ from a plain program's by a relative error of at most 0.0057.
Values may be sent and summed in bfloat16 or wider, within the bound.
A program may use at most 128 MiB of HBM per device.

v0:
```python
import jax
import jax.numpy as jnp
from jax import lax
from jax.sharding import PartitionSpec as P

score_scale = 192.0 ** (-0.5)


def expert_block(chosen, gate_matrix, up_matrix, down_matrix):
    gate_part = jnp.dot(chosen, gate_matrix, preferred_element_type=jnp.float32)
    up_part = jnp.dot(chosen, up_matrix, preferred_element_type=jnp.float32)
    hidden_units = (jax.nn.silu(gate_part) * up_part).astype(jnp.bfloat16)
    return lax.dot_general(
        hidden_units, down_matrix, (((1,), (1,)), ((), ())), preferred_element_type=jnp.float32
    )


def attend_row(query_lat, query_rope, cache_lat, cache_rope, length):
    head_count = query_lat.shape[0]
    rope_width = cache_rope.shape[0]
    scores = lax.dot_general(
        query_lat, cache_lat, (((1,), (1,)), ((), ())), preferred_element_type=jnp.float32
    )
    scores = scores + jnp.dot(
        query_rope.reshape(head_count, rope_width), cache_rope, preferred_element_type=jnp.float32
    )
    scores = scores * score_scale
    positions = jnp.arange(cache_lat.shape[0], dtype=jnp.int32)
    valid = (positions < length)[None, :]
    scores = jnp.where(valid, scores, jnp.float32(-1e30))
    highest = jnp.max(scores, axis=1, keepdims=True)
    weights = jnp.where(valid, jnp.exp(scores - highest), jnp.float32(0.0))
    probs = (weights / jnp.sum(weights, axis=1, keepdims=True)).astype(jnp.bfloat16)
    return jnp.dot(probs, cache_lat, preferred_element_type=jnp.float32).astype(jnp.bfloat16)


def per_device(
    moe_rows,
    expert_ids,
    gate_weights,
    w_gate,
    w_up,
    w_down,
    q_latent,
    q_rope,
    latent_cache,
    rope_cache,
    lengths,
):
    tok_count = moe_rows.shape[0]
    width = moe_rows.shape[1]
    topk_count = expert_ids.shape[1]
    experts = lax.axis_size("dev")
    capacity = min(tok_count, 2 * tok_count * topk_count // experts)
    flat_ids = expert_ids.reshape(-1)
    pair_count = flat_ids.shape[0]
    one_hot = (flat_ids[:, None] == jnp.arange(experts, dtype=jnp.int32)[None, :]).astype(jnp.int32)
    earlier = jnp.cumsum(one_hot, axis=0) - one_hot
    slot_index = jnp.sum(earlier * one_hot, axis=1)
    destination = flat_ids * capacity + slot_index
    source_row = jnp.full((experts * capacity,), tok_count, jnp.int32)
    source_row = source_row.at[destination].set(
        jnp.arange(pair_count, dtype=jnp.int32) // topk_count
    )
    padded_rows = jnp.concatenate([moe_rows, jnp.zeros((1, width), jnp.bfloat16)], axis=0)
    outgoing = padded_rows[source_row].reshape(experts, capacity, width)
    arrived = lax.all_to_all(outgoing, "dev", split_axis=0, concat_axis=0, tiled=True)
    own_rows = arrived.reshape(experts * capacity, width)
    both_rows = lax.all_gather(own_rows, "role", axis=0, tiled=True)
    expert_sum = lax.psum_scatter(
        expert_block(both_rows, w_gate[0], w_up[0], w_down[0]),
        "role",
        scatter_dimension=0,
        tiled=True,
    )
    finished = expert_sum.astype(jnp.bfloat16).reshape(experts, capacity, width)
    returned = lax.all_to_all(finished, "dev", split_axis=0, concat_axis=0, tiled=True)
    flat_back = returned.reshape(experts * capacity, width)
    picked = flat_back[destination].reshape(tok_count, topk_count, width).astype(jnp.float32)
    moe_out = jnp.sum(picked * gate_weights[:, :, None], axis=1).astype(jnp.bfloat16)
    attended = jax.vmap(attend_row)(q_latent, q_rope, latent_cache, rope_cache, lengths)
    return (moe_out, attended)


def solution(mesh):
    placed = (
        P(("role", "dev"), None),
        P(("role", "dev"), None),
        P(("role", "dev"), None),
        P("dev", None, "role"),
        P("dev", None, "role"),
        P("dev", None, "role"),
        P(("role", "dev"), None, None),
        P(("role", "dev"), None),
        P(("role", "dev"), None, None),
        P(("role", "dev"), None, None),
        P(("role", "dev")),
    )
    return jax.shard_map(
        per_device,
        mesh=mesh,
        in_specs=placed,
        out_specs=(P(("role", "dev"), None), P(("role", "dev"), None, None)),
        check_vma=False,
    )
```

profile of v0, /device:TPU:1, one launch (start us, length us, event | category | flops | bytes accessed | tf_op | source)
XLA Modules:
  0.0 223.4 jit_solution(7646429509567561305)
XLA Ops:
  7.2 0.0 copy-start
  7.2 0.0 all-gather.2.cloned.1.call-start
  7.2 0.8 copy.15
  8.1 0.1 eq.29
  8.2 0.1 eq.25
  8.2 0.7 broadcast_multiply_fusion
  9.0 0.6 reduce-window.6
  9.6 0.2 slice_reduce_fusion
  9.8 0.1 copy.14
  9.9 0.1 mul.42
  10.0 0.1 fusion.21
  10.1 1.4 scatter_custom_fusion
  11.5 1.0 concatenate.3
  12.5 4.2 %gather_fusion = bf16[512,3584]{1,0:T(8,128)(2,1)} fusion(bf16[33,3584]{1,0:T(8,128)(2,1)S(1)} %concatenate.3, s32[1024]{0:T(1024)S(1)} %pad_clamp_fusion.1), kind=kCustom, calls=%fused_computation | custom fusion | bytes 7342080 | tf_op jit(solution)/shard_map/gather | solution.py:66
  16.7 57.5 %all_to_all.10 = bf16[64,8,3584]{2,1,0:T(8,128)(2,1)} all-to-all(bf16[64,8,3584]{2,1,0:T(8,128)(2,1)} %bitcast.49), channel_id=1, replica_groups=mesh['role'=2,'dev'=64] {'dev'}, dimensions={0} | all-to-all | bytes 7340032 | tf_op jit(solution)/shard_map/all_to_all | solution.py:67
  74.2 0.0 all-gather.2.cloned.1.call-update
  74.2 0.0 reduce-scatter.2.cloned.1.call-start
  74.3 19.5 %all-gather.2.cloned.1.call-done = bf16[1024,3584]{1,0:T(8,128)(2,1)} async-done(((bf16[512,3584]{1,0:T(8,128)(2,1)}), bf16[1024,3584]{1,0:T(8,128)(2,1)}) %all-gather.2.cloned.1.call-update) | async-done | bytes 7340048 | tf_op jit(solution)/shard_map/all_gather | solution.py:69
  93.8 7.3 %fusion.4 = f32[1024,512]{1,0:T(8,128)S(1)} fusion(bf16[1024,3584]{1,0:T(8,128)(2,1)} %all-gather.2.cloned.1.call-done, bf16[1,3584,512]{2,1,0:T(8,128)(2,1)} %param.15), kind=kOutput, calls=%fused_computation.8 | convolution fusion | flops 3758096384 | bytes 13107200 | tf_op jit(solution)/shard_map/dot_general | solution.py:11
  101.1 15.5 %fusion.2 = f32[1024,3584]{1,0:T(8,128)} fusion(bf16[1,3584,512]{2,1,0:T(8,128)(2,1)} %param.16, f32[1024,512]{1,0:T(8,128)S(1)} %fusion.4, bf16[1024,3584]{1,0:T(8,128)(2,1)} %all-gather.2.cloned.1.call-done, bf16[1,3584,512]{2,1,0:T(8,128)(2,1)} %param.14), kind=kOutput, calls=%fused_computation.6 | convolution fusion | flops 7519338496 | bytes 31457280 | tf_op jit(solution)/shard_map/dot_general | solution.py:13
  116.6 0.0 reduce-scatter.2.cloned.1.call-update
  116.6 28.2 %reduce-scatter.2.cloned.1.call-done = f32[512,3584]{1,0:T(8,128)} async-done(((f32[1024,3584]{1,0:T(8,128)}), f32[512,3584]{1,0:T(8,128)}) %reduce-scatter.2.cloned.1.call-update) | async-done | bytes 7340048 | tf_op jit(solution)/shard_map/reduce_scatter | solution.py:70
  144.8 5.3 %convert_bitcast_fusion = bf16[64,8,3584]{2,1,0:T(8,128)(2,1)} fusion(f32[512,3584]{1,0:T(8,128)} %reduce-scatter.2.cloned.1.call-done), kind=kLoop, calls=%fused_computation.12 | loop fusion | flops 1835008 | bytes 11010048 | tf_op jit(solution)/shard_map/reshape | solution.py:76
  150.1 0.0 copy-start.3
  150.1 0.0 copy-start.2
  150.1 0.0 copy-start.4
  150.1 0.0 copy-start.1
  150.1 10.7 %all-to-all-start.1 = ((bf16[64,8,3584]{2,1,0:T(8,128)(2,1)}), bf16[64,8,3584]{2,1,0:T(8,128)(2,1)}, u32[]{:S(2)}, u32[]{:S(2)}) async-start(bf16[64,8,3584]{2,1,0:T(8,128)(2,1)} %convert_bitcast_fusion), calls=%async_computation.2 | async-start | bytes 7340032 | tf_op jit(solution)/shard_map/all_to_all | solution.py:77
  160.8 0.0 copy-done.3
  160.8 0.1 copy.18
  160.8 0.0 copy-done.2
  160.8 0.1 reshape.93
  161.0 0.0 copy-done.4
  161.0 0.1 iota_compare_fusion.2
  161.1 0.0 copy-done.1
  161.1 6.0 %fusion.27 = f32[4,64,2048]{2,1,0:T(8,128)S(1)} fusion(bf16[4,64,512]{2,1,0:T(8,128)(2,1)S(1)} %copy-done.1, bf16[4,2048,512]{2,1,0:T(8,128)(2,1)} %param.19), kind=kOutput, calls=%fused_computation.47 | convolution fusion | flops 536870912 | bytes 10747904 | tf_op jit(solution)/shard_map/vmap()/dot_general | solution.py:21
  167.1 0.0 copy-done
  167.1 2.4 %fusion.26 = (f32[4,64]{1,0:T(4,128)S(1)}, f32[4,64,2048]{2,1,0:T(8,128)}) fusion(pred[4,2048]{1,0:T(4,128)(4,1)S(1)} %iota_compare_fusion.2, f32[4,64,2048]{2,1,0:T(8,128)S(1)} %fusion.27, bf16[4,64,64]{2,1,0:T(8,128)(2,1)S(1)} %reshape.93, bf16[4,64,2048]{2,1,0:T(8,128)(2,1)S(1)} %copy-done), kind=kOutput, calls=%fused_computation.46 | convolution fusion | flops 70256640 | bytes 5284864 | tf_op jit(solution)/shard_map/vmap()/sub | solution.py:32
  169.4 6.3 %convolution_convert_fusion = bf16[4,64,512]{2,1,0:T(8,128)(2,1)} fusion(bf16[4,2048,512]{2,1,0:T(8,128)(2,1)} %param.19, f32[4,64,2048]{2,1,0:T(8,128)} %get-tuple-element.3, f32[4,64]{1,0:T(4,128)S(1)} %get-tuple-element.2), kind=kOutput, calls=%fused_computation.21 | convolution fusion | flops 538050560 | bytes 10748928 | tf_op jit(solution)/shard_map/vmap()/dot_general | solution.py:34
  175.8 32.6 %all-to-all-done.1 = bf16[64,8,3584]{2,1,0:T(8,128)(2,1)} async-done(((bf16[64,8,3584]{2,1,0:T(8,128)(2,1)}), bf16[64,8,3584]{2,1,0:T(8,128)(2,1)}, u32[]{:S(2)}, u32[]{:S(2)}) %all-to-all-start.1) | async-done | bytes 3670048 | tf_op jit(solution)/shard_map/all_to_all | solution.py:77
  208.4 6.0 %gather_fusion.1 = bf16[256,3584]{1,0:T(8,128)(2,1)S(1)} fusion(bf16[512,3584]{1,0:T(8,128)(2,1)} %bitcast.9, s32[1024]{0:T(1024)S(1)} %pad_clamp_fusion), kind=kCustom, calls=%fused_computation.1 | custom fusion | bytes 3671040 | tf_op jit(solution)/shard_map/gather | solution.py:79
  214.5 2.1 fusion.1
  (8 shorter events, 0.1 us)
Async XLA Ops:
  7.2 159.9 %copy-start = (bf16[4,64,2048]{2,1,0:T(8,128)(2,1)S(1)}, bf16[4,64,2048]{2,1,0:T(8,128)(2,1)}, u32[]{:S(2)}) copy-start(bf16[4,64,2048]{2,1,0:T(8,128)(2,1)} %param.20) | copy-start | bytes 3145732
  7.2 86.6 %all-gather.2.cloned.1.call-start = ((), (), s32[]{:S(2)}) async-start(), calls=%async_computation.3 | async-start | bytes 11010048 | tf_op jit(solution)/shard_map/all_gather | solution.py:69
  74.2 70.5 %reduce-scatter.2.cloned.1.call-start = ((), (), s32[]{:S(2)}) async-start(), calls=%async_computation.4 | async-start | bytes 22020096 | tf_op jit(solution)/shard_map/reduce_scatter | solution.py:70
  150.1 10.7 %copy-start.3 = (f32[32,8]{0,1:T(8,128)S(1)}, f32[32,8]{0,1:T(8,128)}, u32[]{:S(2)}) copy-start(f32[32,8]{0,1:T(8,128)} %param.13) | copy-start | bytes 3076
  150.1 10.8 %copy-start.2 = (bf16[4,4096]{1,0:T(4,128)(2,1)S(1)}, bf16[4,4096]{1,0:T(4,128)(2,1)}, u32[]{:S(2)}) copy-start(bf16[4,4096]{1,0:T(4,128)(2,1)} %param.18) | copy-start | bytes 98308
  150.1 10.9 %copy-start.4 = (s32[4]{0:T(128)S(1)}, s32[4]{0:T(128)}, u32[]{:S(2)}) copy-start(s32[4]{0:T(128)} %param.21) | copy-start | bytes 52
  150.1 11.0 %copy-start.1 = (bf16[4,64,512]{2,1,0:T(8,128)(2,1)S(1)}, bf16[4,64,512]{2,1,0:T(8,128)(2,1)}, u32[]{:S(2)}) copy-start(bf16[4,64,512]{2,1,0:T(8,128)(2,1)} %param.17) | copy-start | bytes 786436
  150.1 58.3 %all-to-all-start.1 = ((bf16[64,8,3584]{2,1,0:T(8,128)(2,1)}), bf16[64,8,3584]{2,1,0:T(8,128)(2,1)}, u32[]{:S(2)}, u32[]{:S(2)}) async-start(bf16[64,8,3584]{2,1,0:T(8,128)(2,1)} %convert_bitcast_fusion), calls=%async_computation.2 | async-start | bytes 7340032 | tf_op jit(solution)/shard_map/all_to_all | solution.py:77
Sparse Core Ops, SparseCore 0:
  74.4 19.3 all-gather.1
  116.7 28.0 reduce-scatter.1
where the time goes:
time: 224 us; the launch traced here: 223 us
  waiting for transfers between devices  80.4 us (36%)
  blocking collectives  57.5 us (26%)
  matrix products  37.5 us (17%)
  local copies, waits for them, and re-layouts  14.2 us (6%)
  between operations  14.2 us (6%)
  starting transfers between devices  10.8 us (5%)
  other arithmetic  8.97 us (4%)
    all_to_all x1, blocking collectives, per_device(): lax.all_to_all(outgoing, 'dev', split_axis=0, concat_axis=0, tiled=True)  57.5 us
    all_to_all x1, waiting for transfers between devices, per_device(): lax.all_to_all(finished, 'dev', split_axis=0, concat_axis=0, tiled=True)  32.6 us
    reduce_scatter x1, waiting for transfers between devices, per_device(): lax.psum_scatter(expert_block(both_rows, w_gate[0], w_up[0], w_down[0]),...  28.2 us
    all_gather x1, waiting for transfers between devices, per_device(): both_rows = lax.all_gather(own_rows, 'role', axis=0, tiled=True)  19.5 us
    dot_general x1, matrix products, expert_block(): lax.dot_general(hidden_units, down_matrix, (((1,), (1,)), ((), ())), pref...  15.5 us
    all_to_all x1, starting transfers between devices, per_device(): lax.all_to_all(finished, 'dev', split_axis=0, concat_axis=0, tiled=True)  10.7 us
    dot_general x1, matrix products, expert_block(): up_part = jnp.dot(chosen, up_matrix, preferred_element_type=jnp.float32)  7.29 us
    dot_general x1, matrix products, attend_row(): jnp.dot(probs, cache_lat, preferred_element_type=jnp.float32)  6.34 us
  transfers between devices with their start and end apart: 3, of which 3 were waited for; matrix products, arithmetic and copies ran while one was open for 7% of the time, Pallas kernels for 0%

commit v1 on v0

--- a/solution.py
+++ b/solution.py
@@ -66,7 +66,11 @@
     outgoing = padded_rows[source_row].reshape(experts, capacity, width)
     arrived = lax.all_to_all(outgoing, "dev", split_axis=0, concat_axis=0, tiled=True)
     own_rows = arrived.reshape(experts * capacity, width)
-    both_rows = lax.all_gather(own_rows, "role", axis=0, tiled=True)
+    size = lax.axis_size("role")
+    repeats = [size if d == 0 else 1 for d in range(own_rows.ndim)]
+    both_rows = lax.all_to_all(
+        jnp.tile(own_rows, repeats), "role", split_axis=0, concat_axis=0, tiled=True
+    )
     expert_sum = lax.psum_scatter(
         expert_block(both_rows, w_gate[0], w_up[0], w_down[0]),
         "role",

time: 224 us -> 211 us (0.942)
  waiting for transfers between devices: 80.4 us -> 55.9 us
  blocking collectives: 57.5 us -> 69.3 us
  local copies, waits for them, and re-layouts: 14.2 us -> 17.6 us
  matrix products: 37.5 us -> 34.1 us
    all_gather x1 -> x0, waiting for transfers between devices: 19.5 us -> none  [per_device(): both_rows = lax.all_gather(own_rows, 'role', axis=0, tiled=True)]
    all_to_all x0 -> x1, blocking collectives: none -> 11.9 us  [per_device(): lax.all_to_all(jnp.tile(own_rows, repeats), 'role', split_axis=0, concat_...]
    reduce_scatter x1, waiting for transfers between devices: 28.2 us -> 23.2 us  [per_device(): lax.psum_scatter(expert_block(both_rows, w_gate[0], w_up[0], w_down[0]),...]
    dot_general x1, matrix products: 7.29 us -> 3.93 us  [expert_block(): up_part = jnp.dot(chosen, up_matrix, preferred_element_type=jnp.float32)]
    unnamed x12 -> x16, local copies, waits for them, and re-layouts: 0.94 us -> 3.89 us
  transfers between devices with their start and end apart: 3 -> 2, of which waited for: 3 -> 2; matrix products, arithmetic and copies ran while one was open for 7% -> 7% of each run, Pallas kernels for 0% -> 0%
where the time goes in v1:
time: 211 us
  blocking collectives  69.3 us (33%)
  waiting for transfers between devices  55.9 us (26%)
  matrix products  34.1 us (16%)
  local copies, waits for them, and re-layouts  17.6 us (8%)
  between operations  14.2 us (7%)
  starting transfers between devices  10.7 us (5%)
  other arithmetic  8.97 us (4%)
    all_to_all x1, blocking collectives, per_device(): lax.all_to_all(outgoing, 'dev', split_axis=0, concat_axis=0, tiled=True)  57.4 us
    all_to_all x1, waiting for transfers between devices, per_device(): lax.all_to_all(finished, 'dev', split_axis=0, concat_axis=0, tiled=True)  32.6 us
    reduce_scatter x1, waiting for transfers between devices, per_device(): lax.psum_scatter(expert_block(both_rows, w_gate[0], w_up[0], w_down[0]),...  23.2 us
    dot_general x1, matrix products, expert_block(): lax.dot_general(hidden_units, down_matrix, (((1,), (1,)), ((), ())), pref...  15.5 us
    all_to_all x1, blocking collectives, per_device(): lax.all_to_all(jnp.tile(own_rows, repeats), 'role', split_axis=0, concat_...  11.9 us
    all_to_all x1, starting transfers between devices, per_device(): lax.all_to_all(finished, 'dev', split_axis=0, concat_axis=0, tiled=True)  10.7 us
    dot_general x1, matrix products, attend_row(): jnp.dot(probs, cache_lat, preferred_element_type=jnp.float32)  6.34 us
    gather x1, local copies, waits for them, and re-layouts, per_device(): flat_back[destination].reshape(tok_count, topk_count, width)  6.04 us
  transfers between devices with their start and end apart: 2, of which 2 were waited for; matrix products, arithmetic and copies ran while one was open for 7% of the time, Pallas kernels for 0%

profile of v1, /device:TPU:1, one launch (start us, length us, event | category | flops | bytes accessed | tf_op | source)
XLA Modules:
  0.0 210.7 jit_solution(7105587924871440470)
XLA Ops:
  7.2 0.0 copy-start
  7.2 0.0 reduce-scatter.2.cloned.1.call-start
  7.2 0.8 copy.15
  8.1 0.1 eq.29
  8.2 0.1 eq.25
  8.2 0.7 broadcast_multiply_fusion
  9.0 0.6 reduce-window.6
  9.6 0.2 slice_reduce_fusion
  9.8 0.1 copy.14
  9.9 0.1 mul.42
  10.0 0.1 fusion.21
  10.1 1.4 scatter_custom_fusion
  11.5 1.0 concatenate.3
  12.5 4.2 %gather_fusion = bf16[512,3584]{1,0:T(8,128)(2,1)} fusion(bf16[33,3584]{1,0:T(8,128)(2,1)S(1)} %concatenate.3, s32[1024]{0:T(1024)S(1)} %pad_clamp_fusion.1), kind=kCustom, calls=%fused_computation | custom fusion | bytes 7342080 | tf_op jit(solution)/shard_map/gather | solution.py:66
  16.6 57.4 %all_to_all.19 = bf16[64,8,3584]{2,1,0:T(8,128)(2,1)S(1)} all-to-all(bf16[64,8,3584]{2,1,0:T(8,128)(2,1)} %bitcast.50), channel_id=1, replica_groups=mesh['role'=2,'dev'=64] {'dev'}, dimensions={0} | all-to-all | bytes 7340032 | tf_op jit(solution)/shard_map/all_to_all | solution.py:67
  74.1 0.5 tile.9
  74.5 0.0 copy-start.6
  74.5 11.9 %all_to_all.20 = bf16[2,512,3584]{2,1,0:T(8,128)(2,1)S(1)} all-to-all(bf16[2,512,3584]{2,1,0:T(8,128)(2,1)S(1)} %tile.9), channel_id=1, replica_groups=mesh['role'=2,'dev'=64] {'role'}, dimensions={0} | all-to-all | bytes 14680064 | tf_op jit(solution)/shard_map/all_to_all | solution.py:71
  86.4 0.0 copy-start.1
  86.5 2.9 %copy-done.1 = bf16[2,512,3584]{2,1,0:T(8,128)(2,1)} copy-done((bf16[2,512,3584]{2,1,0:T(8,128)(2,1)}, bf16[2,512,3584]{2,1,0:T(8,128)(2,1)S(1)}, u32[]{:S(2)}) %copy-start.1) | copy-done | bytes 7340056
  89.4 0.0 copy-done.6
  89.4 3.9 %fusion.4 = f32[1024,512]{1,0:T(8,128)S(1)} fusion(bf16[1024,3584]{1,0:T(8,128)(2,1)S(1)} %bitcast.52, bf16[1,3584,512]{2,1,0:T(8,128)(2,1)S(1)} %copy-done.6), kind=kOutput, calls=%fused_computation.8 | convolution fusion | flops 3758096384 | bytes 13107200 | tf_op jit(solution)/shard_map/dot_general | solution.py:11
  93.3 15.5 %fusion.2 = f32[1024,3584]{1,0:T(8,128)} fusion(bf16[1,3584,512]{2,1,0:T(8,128)(2,1)} %param.16, f32[1024,512]{1,0:T(8,128)S(1)} %fusion.4, bf16[1024,3584]{1,0:T(8,128)(2,1)} %bitcast.53, bf16[1,3584,512]{2,1,0:T(8,128)(2,1)} %param.14), kind=kOutput, calls=%fused_computation.6 | convolution fusion | flops 7519338496 | bytes 31457280 | tf_op jit(solution)/shard_map/dot_general | solution.py:13
  108.8 0.0 reduce-scatter.2.cloned.1.call-update
  108.8 23.2 %reduce-scatter.2.cloned.1.call-done = f32[512,3584]{1,0:T(8,128)} async-done(((f32[1024,3584]{1,0:T(8,128)}), f32[512,3584]{1,0:T(8,128)}) %reduce-scatter.2.cloned.1.call-update) | async-done | bytes 7340048 | tf_op jit(solution)/shard_map/reduce_scatter | solution.py:74
  132.1 5.3 %convert_bitcast_fusion = bf16[64,8,3584]{2,1,0:T(8,128)(2,1)} fusion(f32[512,3584]{1,0:T(8,128)} %reduce-scatter.2.cloned.1.call-done), kind=kLoop, calls=%fused_computation.12 | loop fusion | flops 1835008 | bytes 11010048 | tf_op jit(solution)/shard_map/reshape | solution.py:80
  137.3 0.0 copy-start.4
  137.3 0.0 copy-start.3
  137.3 0.0 copy-start.5
  137.3 0.0 copy-start.2
  137.3 10.7 %all-to-all-start.2 = ((bf16[64,8,3584]{2,1,0:T(8,128)(2,1)}), bf16[64,8,3584]{2,1,0:T(8,128)(2,1)}, u32[]{:S(2)}, u32[]{:S(2)}) async-start(bf16[64,8,3584]{2,1,0:T(8,128)(2,1)} %convert_bitcast_fusion), calls=%async_computation.3 | async-start | bytes 7340032 | tf_op jit(solution)/shard_map/all_to_all | solution.py:81
  148.0 0.0 copy-done.4
  148.0 0.1 copy.18
  148.1 0.0 copy-done.3
  148.1 0.1 reshape.96
  148.2 0.0 copy-done.5
  148.3 0.1 iota_compare_fusion.2
  148.3 0.0 copy-done.2
  148.4 6.0 %fusion.27 = f32[4,64,2048]{2,1,0:T(8,128)S(1)} fusion(bf16[4,64,512]{2,1,0:T(8,128)(2,1)S(1)} %copy-done.2, bf16[4,2048,512]{2,1,0:T(8,128)(2,1)} %param.19), kind=kOutput, calls=%fused_computation.47 | convolution fusion | flops 536870912 | bytes 10747904 | tf_op jit(solution)/shard_map/vmap()/dot_general | solution.py:21
  154.4 0.0 copy-done
  154.4 2.3 %fusion.26 = (f32[4,64]{1,0:T(4,128)S(1)}, f32[4,64,2048]{2,1,0:T(8,128)}) fusion(pred[4,2048]{1,0:T(4,128)(4,1)S(1)} %iota_compare_fusion.2, f32[4,64,2048]{2,1,0:T(8,128)S(1)} %fusion.27, bf16[4,64,64]{2,1,0:T(8,128)(2,1)S(1)} %reshape.96, bf16[4,64,2048]{2,1,0:T(8,128)(2,1)S(1)} %copy-done), kind=kOutput, calls=%fused_computation.46 | convolution fusion | flops 70256640 | bytes 5284864 | tf_op jit(solution)/shard_map/vmap()/sub | solution.py:32
  156.7 6.3 %convolution_convert_fusion = bf16[4,64,512]{2,1,0:T(8,128)(2,1)} fusion(bf16[4,2048,512]{2,1,0:T(8,128)(2,1)} %param.19, f32[4,64,2048]{2,1,0:T(8,128)} %get-tuple-element.3, f32[4,64]{1,0:T(4,128)S(1)} %get-tuple-element.2), kind=kOutput, calls=%fused_computation.21 | convolution fusion | flops 538050560 | bytes 10748928 | tf_op jit(solution)/shard_map/vmap()/dot_general | solution.py:34
  163.1 32.6 %all-to-all-done.2 = bf16[64,8,3584]{2,1,0:T(8,128)(2,1)} async-done(((bf16[64,8,3584]{2,1,0:T(8,128)(2,1)}), bf16[64,8,3584]{2,1,0:T(8,128)(2,1)}, u32[]{:S(2)}, u32[]{:S(2)}) %all-to-all-start.2) | async-done | bytes 3670048 | tf_op jit(solution)/shard_map/all_to_all | solution.py:81
  195.7 6.0 %gather_fusion.1 = bf16[256,3584]{1,0:T(8,128)(2,1)S(1)} fusion(bf16[512,3584]{1,0:T(8,128)(2,1)} %bitcast.10, s32[1024]{0:T(1024)S(1)} %pad_clamp_fusion), kind=kCustom, calls=%fused_computation.1 | custom fusion | bytes 3671040 | tf_op jit(solution)/shard_map/gather | solution.py:83
  201.7 2.1 %fusion.1 = bf16[32,3584]{1,0:T(8,128)(2,1)} fusion(bf16[256,3584]{1,0:T(8,128)(2,1)S(1)} %gather_fusion.1, f32[32,8]{1,0:T(8,128)S(1)} %copy.18), kind=kLoop, calls=%fused_computation.5 | loop fusion | flops 2637824 | bytes 2065408 | tf_op jit(solution)/shard_map/reduce_sum | solution.py:84
  (8 shorter events, 0.1 us)
Async XLA Ops:
  7.2 147.2 %copy-start = (bf16[4,64,2048]{2,1,0:T(8,128)(2,1)S(1)}, bf16[4,64,2048]{2,1,0:T(8,128)(2,1)}, u32[]{:S(2)}) copy-start(bf16[4,64,2048]{2,1,0:T(8,128)(2,1)} %param.20) | copy-start | bytes 3145732
  7.2 124.9 %reduce-scatter.2.cloned.1.call-start = ((), (), s32[]{:S(2)}) async-start(), calls=%async_computation.4 | async-start | bytes 22020096 | tf_op jit(solution)/shard_map/reduce_scatter | solution.py:74
  74.5 14.9 %copy-start.6 = (bf16[1,3584,512]{2,1,0:T(8,128)(2,1)S(1)}, bf16[1,3584,512]{2,1,0:T(8,128)(2,1)}, u32[]{:S(2)}) copy-start(bf16[1,3584,512]{2,1,0:T(8,128)(2,1)} %param.15) | copy-start | bytes 11010052
  86.4 2.9 %copy-start.1 = (bf16[2,512,3584]{2,1,0:T(8,128)(2,1)}, bf16[2,512,3584]{2,1,0:T(8,128)(2,1)S(1)}, u32[]{:S(2)}) copy-start(bf16[2,512,3584]{2,1,0:T(8,128)(2,1)S(1)} %all_to_all.20) | copy-start | bytes 22020100
  137.3 10.7 %copy-start.4 = (f32[32,8]{0,1:T(8,128)S(1)}, f32[32,8]{0,1:T(8,128)}, u32[]{:S(2)}) copy-start(f32[32,8]{0,1:T(8,128)} %param.13) | copy-start | bytes 3076
  137.3 10.8 %copy-start.3 = (bf16[4,4096]{1,0:T(4,128)(2,1)S(1)}, bf16[4,4096]{1,0:T(4,128)(2,1)}, u32[]{:S(2)}) copy-start(bf16[4,4096]{1,0:T(4,128)(2,1)} %param.18) | copy-start | bytes 98308
  137.3 10.9 %copy-start.5 = (s32[4]{0:T(128)S(1)}, s32[4]{0:T(128)}, u32[]{:S(2)}) copy-start(s32[4]{0:T(128)} %param.21) | copy-start | bytes 52
  137.3 11.0 %copy-start.2 = (bf16[4,64,512]{2,1,0:T(8,128)(2,1)S(1)}, bf16[4,64,512]{2,1,0:T(8,128)(2,1)}, u32[]{:S(2)}) copy-start(bf16[4,64,512]{2,1,0:T(8,128)(2,1)} %param.17) | copy-start | bytes 786436
  137.3 58.3 %all-to-all-start.2 = ((bf16[64,8,3584]{2,1,0:T(8,128)(2,1)}), bf16[64,8,3584]{2,1,0:T(8,128)(2,1)}, u32[]{:S(2)}, u32[]{:S(2)}) async-start(bf16[64,8,3584]{2,1,0:T(8,128)(2,1)} %convert_bitcast_fusion), calls=%async_computation.3 | async-start | bytes 7340032 | tf_op jit(solution)/shard_map/all_to_all | solution.py:81
Sparse Core Ops, SparseCore 0:
  108.9 23.0 reduce-scatter.1
